TPU v7x, 32 devices: a whole 2x2x4 slice. The times are simulated.
32 devices in a mesh: ctx: 8 (over z, x), head: 4 (over y, core).
Axes of the slice: x: 2, y: 2, z: 4, core: 2. Of those that a mesh axis runs over, the one named last changes fastest.
Arguments:
- positions: int32 [128], replicated, may hold values from 1 to 8191, as said below
- mla_queries: bfloat16 [128, 128, 576], P(None, 'head'), may hold values from -5000 to 5000
- latent_keys: bfloat16 [8192, 576], P('ctx'), may hold values from -18 to 18
- index_queries: bfloat16 [128, 64, 128], P(None, 'head'), may hold values from -64 to 64
- index_keys: bfloat16 [8192, 128], P('ctx'), may hold values from -18 to 18
- head_weights: float32 [128, 64], P(None, 'head'), may hold values from -4 to 4
Outputs:
- grad_queries: float32 [128, 64, 128], P('ctx', 'head')
- grad_keys: float32 [8192, 128], P(('ctx', 'head'))
- grad_weights: float32 [128, 64], P('ctx', 'head')
Inputs may be any that keep to these rules, and one draw needn't show every extreme that they name: Each query sees the keys at positions 0 to its own position.
All inputs are finite; a program needn't handle non-finite values.
Results may differ from a plain program's by a relative error of at most 0.0045.
Values may be sent and summed in bfloat16 or wider, within the bound.
A program may use at most 128 MiB of HBM per device.

v0:
```python
import math
import jax
import jax.numpy as jnp
from jax import lax
from jax.sharding import PartitionSpec as P

HEADS = 128
QK_HEAD = 192
masked_value = -1e30


def masked_highest(values, allowed):
    return jnp.max(jnp.where(allowed, values, masked_value), axis=-1)


def shifted_exp(values, allowed, highest):
    return jnp.where(allowed, jnp.exp(values - highest[..., None]), 0.0)


def local(positions, mla_queries, latent_keys, index_queries, index_keys, head_weights):
    rows = latent_keys.shape[0]
    key_pos = lax.axis_index("ctx") * rows + jnp.arange(rows, dtype=jnp.int32)
    allowed = key_pos[None, :] <= positions[:, None]
    scores = jnp.einsum(
        "thd,sd->hts", mla_queries, latent_keys, preferred_element_type=jnp.float32
    ) * (1.0 / math.sqrt(QK_HEAD))
    head_mask = allowed[None]
    highest = lax.pmax(masked_highest(scores, head_mask), "ctx")
    exponent = shifted_exp(scores, head_mask, highest)
    totals = lax.psum(jnp.sum(exponent, axis=-1), "ctx")
    factor = 1.0 / totals
    mla_part = jnp.sum(exponent * factor[..., None], axis=0)
    inner = jnp.einsum("tjd,sd->tjs", index_queries, index_keys, preferred_element_type=jnp.float32)
    active = jnp.maximum(inner, 0.0)
    logit_part = jnp.einsum("tj,tjs->ts", head_weights, active, precision=lax.Precision.HIGHEST)
    target, logits = (
        lax.psum_scatter(mla_part, "head", scatter_dimension=0, tiled=True),
        lax.psum_scatter(logit_part, "head", scatter_dimension=0, tiled=True),
    )
    share = target.shape[0]
    row_mask = lax.dynamic_slice_in_dim(allowed, lax.axis_index("head") * share, share, 0)
    target = target / HEADS
    index_high = lax.pmax(masked_highest(logits, row_mask), "ctx")
    index_exp = shifted_exp(logits, row_mask, index_high)
    index_sum = lax.psum(jnp.sum(index_exp, axis=-1), "ctx")
    index_factor = 1.0 / index_sum
    predicted = index_exp * index_factor[:, None]
    gradient = jnp.where(
        row_mask, math.sqrt(rows * lax.axis_size("ctx")) * (predicted - target), 0.0
    ).astype(jnp.bfloat16)
    gradient = lax.all_gather(gradient, "head", axis=0, tiled=True)
    grad_float = gradient.astype(jnp.float32)
    weight_part = jnp.einsum("ts,tjs->tj", grad_float, active, precision=lax.Precision.HIGHEST)
    delta = jnp.where(inner > 0, grad_float[:, None, :] * head_weights[:, :, None], 0.0).astype(
        jnp.bfloat16
    )
    query_part = jnp.einsum("tjs,sd->tjd", delta, index_keys, preferred_element_type=jnp.float32)
    grad_queries, grad_weights = (
        lax.psum_scatter(query_part, "ctx", scatter_dimension=0, tiled=True),
        lax.psum_scatter(weight_part, "ctx", scatter_dimension=0, tiled=True),
    )
    grad_keys = lax.psum_scatter(
        jnp.einsum("tjs,tjd->sd", delta, index_queries, preferred_element_type=jnp.float32),
        "head",
        scatter_dimension=0,
        tiled=True,
    )
    return (grad_queries, grad_keys, grad_weights)


def solution(mesh):
    in_specs = (
        P(),
        P(None, "head", None),
        P("ctx", None),
        P(None, "head", None),
        P("ctx", None),
        P(None, "head"),
    )
    out_specs = (P("ctx", "head", None), P(("ctx", "head"), None), P("ctx", "head"))
    return jax.shard_map(local, mesh=mesh, in_specs=in_specs, out_specs=out_specs, check_vma=False)
```

profile of v0, /device:TPU:0, one launch (start us, length us, event | category | flops | bytes accessed | tf_op | source)
XLA Modules:
  0.0 318.5 jit_solution(9850725890422266074)
XLA Ops:
  7.2 0.0 copy-start
  7.2 0.0 copy-start.5
  7.2 0.0 reduce-scatter.16.cloned.1.call-start
  7.2 9.4 %broadcast_maximum_fusion = (f32[128,16,1024]{2,0,1:T(8,128)}, f32[128,1024]{1,0:T(8,128)}, f32[128,16,1024]{2,0,1:T(8,128)}) fusion(f32[128,16]{0,1:T(8,128)} %param.11, bf16[1024,128]{1,0:T(8,128)(2,1)} %param.10, bf16[128,16,128]{2,1,0:T(8,128)(2,1)} %param.9), kind=kOutput, calls=%fused_computation.24 | convolution fusion | flops 543031296 | bytes 18096128 | tf_op jit(solution)/shard_map/tjd,sd->tjs/dot_general | solution.py:33
  16.6 0.0 reduce-scatter.16.cloned.1.call-update
  16.6 0.0 reduce-scatter.18.cloned.1.call-start
  16.7 0.0 copy-done.5
  16.7 0.1 broadcast_compare_fusion
  16.9 0.3 copy.27
  17.1 0.0 copy-done
  17.1 13.1 %fusion = (f32[32,128]{1,0:T(8,128)S(1)}, f32[1024,128,32]{1,0,2:T(8,128)}) fusion(pred[128,1024]{0,1:T(8,128)(4,1)S(1)} %copy.27, bf16[128,32,576]{0,2,1:T(8,128)(2,1)} %param.7, bf16[1024,576]{0,1:T(8,128)(2,1)S(1)} %copy-done), kind=kOutput, calls=%fused_computation.2 | convolution fusion | flops 4844417024 | bytes 22822912 | tf_op jit(solution)/shard_map/thd,sd->hts/dot_general | solution.py:24
  30.3 10.9 %reduce-scatter.16.cloned.1.call-done = f32[32,1024]{1,0:T(8,128)} async-done(((f32[128,1024]{1,0:T(8,128)}), f32[32,1024]{1,0:T(8,128)}) %reduce-scatter.16.cloned.1.call-update) | async-done | bytes 131088 | tf_op jit(solution)/shard_map/reduce_scatter | solution.py:38
  41.2 1.0 select_reduce_fusion
  42.2 37.1 %all-reduce.1 = (f32[32,128]{1,0:T(8,128)S(1)}, f32[32]{0:T(128)S(1)}) all-reduce(f32[32,128]{1,0:T(8,128)S(1)} %get-tuple-element.21, f32[32]{0:T(128)S(1)} %select_reduce_fusion), channel_id=1, replica_groups=mesh['ctx'=8,'head'=4] {'ctx'}, use_global_device_ids=true, to_apply=%region_6.7 | all-reduce | flops 4128 | bytes 33024 | tf_op jit(solution)/shard_map/pmax | solution.py:28
  79.3 0.0 copy-start.1
  79.3 9.1 %fusion.3 = f32[32,128]{1,0:T(8,128)S(1)} fusion(f32[1024,128,32]{1,0,2:T(8,128)} %get-tuple-element.22, f32[32,128]{1,0:T(8,128)S(1)} %get-tuple-element.17, pred[128,1024]{0,1:T(8,128)(4,1)S(1)} %copy.27), kind=kLoop, calls=%fused_computation.6 | loop fusion | flops 16773120 | bytes 16941056 | tf_op jit(solution)/shard_map/reduce_sum | solution.py:30
  88.4 0.0 copy-done.1
  88.4 0.2 fusion.28
  88.6 33.0 %all-reduce = (f32[32,128]{1,0:T(8,128)S(1)}, f32[32]{0:T(128)S(1)}) all-reduce(f32[32,128]{1,0:T(8,128)S(1)} %fusion.3, f32[32]{0:T(128)S(1)} %fusion.28), channel_id=1, replica_groups=mesh['ctx'=8,'head'=4] {'ctx'}, use_global_device_ids=true, to_apply=%region_8.9 | all-reduce | flops 4128 | bytes 33024 | tf_op jit(solution)/shard_map/psum | solution.py:30
  121.7 8.0 %multiply_reduce_fusion = f32[128,1024]{0,1:T(8,128)S(1)} fusion(f32[1024,128,32]{1,0,2:T(8,128)} %get-tuple-element.22, f32[32,128]{1,0:T(8,128)S(1)} %broadcast_divide_fusion, f32[32,128]{1,0:T(8,128)S(1)} %get-tuple-element.17, pred[128,1024]{0,1:T(8,128)(4,1)S(1)} %copy.27), kind=kLoop, calls=%fused_computation.5 | loop fusion | flops 20840448 | bytes 17465344 | tf_op jit(solution)/shard_map/reduce_sum | solution.py:32
  129.7 0.0 copy-start.3
  129.7 0.0 copy-start.4
  129.7 1.0 copy.43
  130.7 0.0 reduce-scatter.18.cloned.1.call-update
  130.7 0.2 reduce-scatter.10.cloned.1.call-start
  130.9 4.6 %fusion.8 = u16[128,1024]{1,0:T(8,128)(2,1)S(1)} fusion(f32[128,16,1024]{2,0,1:T(8,128)} %get-tuple-element.23), kind=kLoop, calls=%fused_computation.15 | loop fusion | flops 10354688 | bytes 8650752
  135.6 13.3 %reduce-scatter.18.cloned.1.call-done = f32[32,1024]{1,0:T(8,128)} async-done(((f32[128,1024]{1,0:T(8,128)}), f32[32,1024]{1,0:T(8,128)}) %reduce-scatter.18.cloned.1.call-update) | async-done | bytes 131088 | tf_op jit(solution)/shard_map/reduce_scatter | solution.py:37
  148.8 1.0 select_convert_fusion.5
  149.9 5.8 %all_gather.3 = bf16[128,1024]{1,0:T(8,128)(2,1)S(1)} all-gather(bf16[32,1024]{1,0:T(8,128)(2,1)S(1)} %select_convert_fusion.5), channel_id=1, replica_groups=mesh['ctx'=8,'head'=4] {'head'}, dimensions={0}, use_global_device_ids=true | all-gather | bytes 327680 | tf_op jit(solution)/shard_map/all_gather | solution.py:51
  155.7 0.0 copy-done.3
  155.7 0.0 copy-done.4
  155.7 2.4 fusion.7
  158.1 0.0 copy-start.2
  158.1 0.0 reduce-scatter.10.cloned.1.call-update
  158.1 0.0 reduce-scatter.14.cloned.1.call-start
  158.2 13.6 %fusion.4 = f32[128,1,16]{2,1,0:T(1,128)} fusion(f32[128,16,1024]{2,0,1:T(8,128)} %get-tuple-element.19, bf16[128,1024,1]{1,0,2:T(8,128)(2,1)S(1)} %bitcast.33), kind=kOutput, calls=%fused_computation.9 | convolution fusion | flops 25165824 | bytes 8658944 | tf_op jit(solution)/shard_map/ts,tjs->tj/dot_general | solution.py:53
  171.7 0.0 reduce-scatter.14.cloned.1.call-update
  171.8 0.0 reduce-scatter.12.cloned.1.call-start
  171.8 0.0 copy-done.2
  171.8 2.8 fusion.19
  174.7 0.0 reduce-scatter.12.cloned.1.call-update
  174.7 48.2 %reduce-scatter.10.cloned.1.call-done = f32[16,16,128]{2,0,1:T(8,128)} async-done(((f32[128,16,128]{2,0,1:T(8,128)}), f32[16,16,128]{2,0,1:T(8,128)}) %reduce-scatter.10.cloned.1.call-update) | async-done | bytes 131088 | tf_op jit(solution)/shard_map/reduce_scatter | solution.py:59
  223.0 1.6 copy.31
  224.6 63.7 %reduce-scatter.14.cloned.1.call-done = f32[16,16]{1,0:T(8,128)} async-done(((f32[128,16]{1,0:T(8,128)}), f32[16,16]{1,0:T(8,128)}) %reduce-scatter.14.cloned.1.call-update) | async-done | bytes 1040 | tf_op jit(solution)/shard_map/reduce_scatter | solution.py:60
  288.2 23.7 %reduce-scatter.12.cloned.1.call-done = f32[256,128]{1,0:T(8,128)} async-done(((f32[1024,128]{1,0:T(8,128)}), f32[256,128]{1,0:T(8,128)}) %reduce-scatter.12.cloned.1.call-update) | async-done | bytes 131088 | tf_op jit(solution)/shard_map/reduce_scatter | solution.py:62
  (4 shorter events, 0.1 us)
Async XLA Ops:
  7.2 10.0 %copy-start = (bf16[1024,576]{0,1:T(8,128)(2,1)S(1)}, bf16[1024,576]{0,1:T(8,128)(2,1)}, u32[]{:S(2)}) copy-start(bf16[1024,576]{0,1:T(8,128)(2,1)} %param.8) | copy-start | bytes 3538948
  7.2 9.5 %copy-start.5 = (s32[128]{0:T(128)S(1)}, s32[128]{0:T(128)}, u32[]{:S(2)}) copy-start(s32[128]{0:T(128)} %param.6) | copy-start | bytes 1540
  7.2 34.0 %reduce-scatter.16.cloned.1.call-start = ((), (), s32[]{:S(2)}) async-start(), calls=%async_computation.8 | async-start | bytes 655360 | tf_op jit(solution)/shard_map/reduce_scatter | solution.py:38
  16.6 132.2 %reduce-scatter.18.cloned.1.call-start = ((), (), s32[]{:S(2)}) async-start(), calls=%async_computation.9 | async-start | bytes 655360 | tf_op jit(solution)/shard_map/reduce_scatter | solution.py:37
  79.3 9.1 %copy-start.1 = (f32[32,1024]{1,0:T(8,128)S(1)}, f32[32,1024]{1,0:T(8,128)}, u32[]{:S(2)}) copy-start(f32[32,1024]{1,0:T(8,128)} %reduce-scatter.16.cloned.1.call-done) | copy-start | bytes 393220
  129.7 26.0 %copy-start.3 = (bf16[1024,128]{1,0:T(8,128)(2,1)S(1)}, bf16[1024,128]{1,0:T(8,128)(2,1)}, u32[]{:S(2)}) copy-start(bf16[1024,128]{1,0:T(8,128)(2,1)} %param.10) | copy-start | bytes 786436
  129.7 26.0 %copy-start.4 = (f32[128,16]{0,1:T(8,128)S(1)}, f32[128,16]{0,1:T(8,128)}, u32[]{:S(2)}) copy-start(f32[128,16]{0,1:T(8,128)} %param.11) | copy-start | bytes 24580
  130.7 92.2 %reduce-scatter.10.cloned.1.call-start = ((), (), s32[]{:S(2)}) async-start(), calls=%async_computation.5 | async-start | bytes 1179648 | tf_op jit(solution)/shard_map/reduce_scatter | solution.py:59
  158.1 13.7 %copy-start.2 = (bf16[128,16,128]{2,1,0:T(8,128)(2,1)S(1)}, bf16[128,16,128]{2,1,0:T(8,128)(2,1)}, u32[]{:S(2)}) copy-start(bf16[128,16,128]{2,1,0:T(8,128)(2,1)} %param.9) | copy-start | bytes 1572868
  158.1 130.1 %reduce-scatter.14.cloned.1.call-start = ((), (), s32[]{:S(2)}) async-start(), calls=%async_computation.7 | async-start | bytes 73728 | tf_op jit(solution)/shard_map/reduce_scatter | solution.py:60
  171.8 140.2 %reduce-scatter.12.cloned.1.call-start = ((), (), s32[]{:S(2)}) async-start(), calls=%async_computation.6 | async-start | bytes 655360 | tf_op jit(solution)/shard_map/reduce_scatter | solution.py:62
Sparse Core Ops, SparseCore 0:
  16.8 24.3 reduce-scatter.15
  130.8 17.9 reduce-scatter.17
  158.2 64.6 reduce-scatter.9
  226.8 61.4 reduce-scatter.13
  291.2 20.7 reduce-scatter.11
where the time goes:
time: 319 us; the launch traced here: 318 us
  waiting for transfers between devices  160 us (50%)
  blocking collectives  75.9 us (24%)
  matrix products  41.3 us (13%)
  other arithmetic  24.2 us (8%)
  between operations  13.9 us (4%)
    reduce_scatter x1, waiting for transfers between devices, local(): lax.psum_scatter(weight_part, 'ctx', scatter_dimension=0, tiled=True)  63.7 us
    reduce_scatter x1, waiting for transfers between devices, local(): lax.psum_scatter(query_part, 'ctx', scatter_dimension=0, tiled=True)  48.2 us
    pmax x1, blocking collectives, local(): highest = lax.pmax(masked_highest(scores, head_mask), 'ctx')  37.1 us
    psum x1, blocking collectives, local(): totals = lax.psum(jnp.sum(exponent, axis=-1), 'ctx')  33 us
    reduce_scatter x1, waiting for transfers between devices, local(): lax.psum_scatter(jnp.einsum('tjs,tjd->sd', delta, index_queries, preferre...  23.7 us
    dot_general x1, matrix products, local(): jnp.einsum('ts,tjs->tj', grad_float, active, precision=lax.Precision.HIGH...  13.6 us
    reduce_scatter x1, waiting for transfers between devices, local(): lax.psum_scatter(mla_part, 'head', scatter_dimension=0, tiled=True)  13.3 us
    dot_general x1, matrix products, local(): jnp.einsum('thd,sd->hts', mla_queries, latent_keys, preferred_element_typ...  13.1 us
  transfers between devices with their start and end apart: 5, of which 5 were waited for; matrix products, arithmetic and copies ran while one was open for 11% of the time, Pallas kernels for 0%

commit v1 on v0

--- a/solution.py
+++ b/solution.py
@@ -27,7 +27,7 @@
     head_mask = allowed[None]
     highest = lax.pmax(masked_highest(scores, head_mask), "ctx")
     exponent = shifted_exp(scores, head_mask, highest)
-    totals = lax.psum(jnp.sum(exponent, axis=-1), "ctx")
+    totals = jnp.sum(lax.all_gather(jnp.sum(exponent, axis=-1), "ctx"), axis=0)
     factor = 1.0 / totals
     mla_part = jnp.sum(exponent * factor[..., None], axis=0)
     inner = jnp.einsum("tjd,sd->tjs", index_queries, index_keys, preferred_element_type=jnp.float32)

time: 319 us -> 318 us (level)
  waiting for transfers between devices: 160 us -> 144 us
  blocking collectives: 75.9 us -> 90.5 us
    all_gather x0 -> x1, blocking collectives: none -> 30.5 us  [local(): totals = jnp.sum(lax.all_gather(jnp.sum(exponent, axis=-1), 'ctx'), axis=0)]
    psum x1, blocking collectives: 33 us -> 17.1 us  [local(): index_sum = lax.psum(jnp.sum(index_exp, axis=-1), 'ctx')]
    reduce_scatter x1, waiting for transfers between devices: 13.3 us -> 0.01 us  [local(): lax.psum_scatter(mla_part, 'head', scatter_dimension=0, tiled=True)]
    reduce_sum x1 -> x2, other arithmetic: 9.14 us -> 9.12 us  [local(): totals = jnp.sum(lax.all_gather(jnp.sum(exponent, axis=-1), 'ctx'), axis=0)]
  transfers between devices with their start and end apart: 5 -> 5, of which waited for: 5 -> 4; matrix products, arithmetic and copies ran while one was open for 11% -> 11% of each run, Pallas kernels for 0% -> 0%
where the time goes in v1:
time: 318 us; the launch traced here: 317 us
  waiting for transfers between devices  144 us (45%)
  blocking collectives  90.5 us (28%)
  matrix products  41.3 us (13%)
  other arithmetic  24.2 us (8%)
  between operations  13.9 us (4%)
    reduce_scatter x1, waiting for transfers between devices, local(): lax.psum_scatter(weight_part, 'ctx', scatter_dimension=0, tiled=True)  63.7 us
    reduce_scatter x1, waiting for transfers between devices, local(): lax.psum_scatter(query_part, 'ctx', scatter_dimension=0, tiled=True)  45.9 us
    pmax x1, blocking collectives, local(): highest = lax.pmax(masked_highest(scores, head_mask), 'ctx')  37.1 us
    all_gather x1, blocking collectives, local(): totals = jnp.sum(lax.all_gather(jnp.sum(exponent, axis=-1), 'ctx'), axis=0)  30.5 us
    reduce_scatter x1, waiting for transfers between devices, local(): lax.psum_scatter(jnp.einsum('tjs,tjd->sd', delta, index_queries, preferre...  23.6 us
    psum x1, blocking collectives, local(): index_sum = lax.psum(jnp.sum(index_exp, axis=-1), 'ctx')  17.1 us
    dot_general x1, matrix products, local(): jnp.einsum('ts,tjs->tj', grad_float, active, precision=lax.Precision.HIGH...  13.6 us
    dot_general x1, matrix products, local(): jnp.einsum('thd,sd->hts', mla_queries, latent_keys, preferred_element_typ...  13.1 us
  transfers between devices with their start and end apart: 5, of which 4 were waited for; matrix products, arithmetic and copies ran while one was open for 11% of the time, Pallas kernels for 0%

profile of v1, /device:TPU:0, one launch (start us, length us, event | category | flops | bytes accessed | tf_op | source)
XLA Modules:
  0.0 317.5 jit_solution(14576498308140434938)
XLA Ops:
  7.2 0.0 copy-start
  7.2 0.0 copy-start.5
  7.2 0.0 reduce-scatter.16.cloned.1.call-start
  7.2 9.4 %broadcast_maximum_fusion = (f32[128,16,1024]{2,0,1:T(8,128)}, f32[128,1024]{1,0:T(8,128)}, f32[128,16,1024]{2,0,1:T(8,128)}) fusion(f32[128,16]{0,1:T(8,128)} %param.11, bf16[1024,128]{1,0:T(8,128)(2,1)} %param.10, bf16[128,16,128]{2,1,0:T(8,128)(2,1)} %param.9), kind=kOutput, calls=%fused_computation.24 | convolution fusion | flops 543031296 | bytes 18096128 | tf_op jit(solution)/shard_map/tjd,sd->tjs/dot_general | solution.py:33
  16.6 0.0 reduce-scatter.16.cloned.1.call-update
  16.6 0.0 reduce-scatter.18.cloned.1.call-start
  16.7 0.0 copy-done.5
  16.7 0.1 broadcast_compare_fusion
  16.9 0.3 copy.32
  17.1 0.0 copy-done
  17.1 13.1 %fusion = (f32[32,128]{1,0:T(8,128)S(1)}, f32[1024,128,32]{1,0,2:T(8,128)}) fusion(pred[128,1024]{0,1:T(8,128)(4,1)S(1)} %copy.32, bf16[128,32,576]{0,2,1:T(8,128)(2,1)} %param.7, bf16[1024,576]{0,1:T(8,128)(2,1)S(1)} %copy-done), kind=kOutput, calls=%fused_computation.2 | convolution fusion | flops 4844417024 | bytes 22822912 | tf_op jit(solution)/shard_map/thd,sd->hts/dot_general | solution.py:24
  30.3 10.9 %reduce-scatter.16.cloned.1.call-done = f32[32,1024]{1,0:T(8,128)} async-done(((f32[128,1024]{1,0:T(8,128)}), f32[32,1024]{1,0:T(8,128)}) %reduce-scatter.16.cloned.1.call-update) | async-done | bytes 131088 | tf_op jit(solution)/shard_map/reduce_scatter | solution.py:38
  41.2 1.0 select_reduce_fusion
  42.2 37.1 %all-reduce = (f32[32,128]{1,0:T(8,128)S(1)}, f32[32]{0:T(128)S(1)}) all-reduce(f32[32,128]{1,0:T(8,128)S(1)} %get-tuple-element.22, f32[32]{0:T(128)S(1)} %select_reduce_fusion), channel_id=1, replica_groups=mesh['ctx'=8,'head'=4] {'ctx'}, use_global_device_ids=true, to_apply=%region_6.7 | all-reduce | flops 4128 | bytes 33024 | tf_op jit(solution)/shard_map/pmax | solution.py:28
  79.3 9.1 %fusion.3 = f32[32,128]{1,0:T(8,128)S(1)} fusion(f32[1024,128,32]{1,0,2:T(8,128)} %get-tuple-element.23, f32[32,128]{1,0:T(8,128)S(1)} %get-tuple-element.18, pred[128,1024]{0,1:T(8,128)(4,1)S(1)} %copy.32), kind=kLoop, calls=%fused_computation.6 | loop fusion | flops 16773120 | bytes 16941056 | tf_op jit(solution)/shard_map/reduce_sum | solution.py:30
  88.4 30.5 %all-gather = f32[256,128]{1,0:T(8,128)S(1)} all-gather(f32[32,128]{1,0:T(8,128)S(1)} %fusion.3), channel_id=2, replica_groups=mesh['ctx'=8,'head'=4] {'ctx'}, dimensions={0}, use_global_device_ids=true | all-gather | bytes 147456 | tf_op jit(solution)/shard_map/all_gather | solution.py:30
  118.9 8.0 %multiply_reduce_fusion = f32[128,1024]{0,1:T(8,128)S(1)} fusion(f32[1024,128,32]{1,0,2:T(8,128)} %get-tuple-element.23, f32[32,128]{1,0:T(8,128)S(1)} %broadcast_divide_fusion, f32[32,128]{1,0:T(8,128)S(1)} %get-tuple-element.18, pred[128,1024]{0,1:T(8,128)(4,1)S(1)} %copy.32), kind=kLoop, calls=%fused_computation.5 | loop fusion | flops 20840448 | bytes 17465344 | tf_op jit(solution)/shard_map/reduce_sum | solution.py:32
  126.9 0.0 copy-start.1
  127.0 0.0 copy-start.3
  127.0 0.0 copy-start.4
  127.0 1.0 copy.48
  128.0 0.0 reduce-scatter.18.cloned.1.call-update
  128.0 0.2 reduce-scatter.10.cloned.1.call-start
  128.2 4.6 %fusion.8 = u16[128,1024]{1,0:T(8,128)(2,1)S(1)} fusion(f32[128,16,1024]{2,0,1:T(8,128)} %get-tuple-element.24), kind=kLoop, calls=%fused_computation.15 | loop fusion | flops 10354688 | bytes 8650752
  132.8 0.0 copy-done.1
  132.9 0.2 fusion.28
  133.1 17.1 %psum.7 = f32[32]{0:T(128)S(1)} all-reduce(f32[32]{0:T(128)S(1)} %fusion.28), channel_id=1, replica_groups=mesh['ctx'=8,'head'=4] {'ctx'}, use_global_device_ids=true, to_apply=%region_4.5 | all-reduce | flops 32 | bytes 256 | tf_op jit(solution)/shard_map/psum | solution.py:45
  150.2 0.0 reduce-scatter.18.cloned.1.call-done
  150.2 1.0 select_convert_fusion.5
  151.2 5.8 %all_gather.11 = bf16[128,1024]{1,0:T(8,128)(2,1)S(1)} all-gather(bf16[32,1024]{1,0:T(8,128)(2,1)S(1)} %select_convert_fusion.5), channel_id=1, replica_groups=mesh['ctx'=8,'head'=4] {'head'}, dimensions={0}, use_global_device_ids=true | all-gather | bytes 327680 | tf_op jit(solution)/shard_map/all_gather | solution.py:51
  157.1 0.0 copy-done.3
  157.1 0.0 copy-done.4
  157.1 2.4 fusion.7
  159.5 0.0 copy-start.2
  159.5 0.0 reduce-scatter.10.cloned.1.call-update
  159.5 0.0 reduce-scatter.14.cloned.1.call-start
  159.5 13.6 %fusion.4 = f32[128,1,16]{2,1,0:T(1,128)} fusion(f32[128,16,1024]{2,0,1:T(8,128)} %get-tuple-element.20, bf16[128,1024,1]{1,0,2:T(8,128)(2,1)S(1)} %bitcast.34), kind=kOutput, calls=%fused_computation.9 | convolution fusion | flops 25165824 | bytes 8658944 | tf_op jit(solution)/shard_map/ts,tjs->tj/dot_general | solution.py:53
  173.1 0.0 reduce-scatter.14.cloned.1.call-update
  173.1 0.0 reduce-scatter.12.cloned.1.call-start
  173.2 0.0 copy-done.2
  173.2 2.8 fusion.19
  176.1 0.0 reduce-scatter.12.cloned.1.call-update
  176.1 45.9 %reduce-scatter.10.cloned.1.call-done = f32[16,16,128]{2,0,1:T(8,128)} async-done(((f32[128,16,128]{2,0,1:T(8,128)}), f32[16,16,128]{2,0,1:T(8,128)}) %reduce-scatter.10.cloned.1.call-update) | async-done | bytes 131088 | tf_op jit(solution)/shard_map/reduce_scatter | solution.py:59
  222.0 1.6 copy.36
  223.6 63.7 %reduce-scatter.14.cloned.1.call-done = f32[16,16]{1,0:T(8,128)} async-done(((f32[128,16]{1,0:T(8,128)}), f32[16,16]{1,0:T(8,128)}) %reduce-scatter.14.cloned.1.call-update) | async-done | bytes 1040 | tf_op jit(solution)/shard_map/reduce_scatter | solution.py:60
  287.3 23.6 %reduce-scatter.12.cloned.1.call-done = f32[256,128]{1,0:T(8,128)} async-done(((f32[1024,128]{1,0:T(8,128)}), f32[256,128]{1,0:T(8,128)}) %reduce-scatter.12.cloned.1.call-update) | async-done | bytes 131088 | tf_op jit(solution)/shard_map/reduce_scatter | solution.py:62
  (5 shorter events, 0.1 us)
Async XLA Ops:
  7.2 10.0 %copy-start = (bf16[1024,576]{0,1:T(8,128)(2,1)S(1)}, bf16[1024,576]{0,1:T(8,128)(2,1)}, u32[]{:S(2)}) copy-start(bf16[1024,576]{0,1:T(8,128)(2,1)} %param.8) | copy-start | bytes 3538948
  7.2 9.5 %copy-start.5 = (s32[128]{0:T(128)S(1)}, s32[128]{0:T(128)}, u32[]{:S(2)}) copy-start(s32[128]{0:T(128)} %param.6) | copy-start | bytes 1540
  7.2 34.0 %reduce-scatter.16.cloned.1.call-start = ((), (), s32[]{:S(2)}) async-start(), calls=%async_computation.8 | async-start | bytes 655360 | tf_op jit(solution)/shard_map/reduce_scatter | solution.py:38
  16.6 133.6 %reduce-scatter.18.cloned.1.call-start = ((), (), s32[]{:S(2)}) async-start(), calls=%async_computation.9 | async-start | bytes 655360 | tf_op jit(solution)/shard_map/reduce_scatter | solution.py:37
  126.9 5.9 %copy-start.1 = (f32[32,1024]{1,0:T(8,128)S(1)}, f32[32,1024]{1,0:T(8,128)}, u32[]{:S(2)}) copy-start(f32[32,1024]{1,0:T(8,128)} %reduce-scatter.16.cloned.1.call-done) | copy-start | bytes 393220
  127.0 30.1 %copy-start.3 = (bf16[1024,128]{1,0:T(8,128)(2,1)S(1)}, bf16[1024,128]{1,0:T(8,128)(2,1)}, u32[]{:S(2)}) copy-start(bf16[1024,128]{1,0:T(8,128)(2,1)} %param.10) | copy-start | bytes 786436
  127.0 30.1 %copy-start.4 = (f32[128,16]{0,1:T(8,128)S(1)}, f32[128,16]{0,1:T(8,128)}, u32[]{:S(2)}) copy-start(f32[128,16]{0,1:T(8,128)} %param.11) | copy-start | bytes 24580
  128.0 94.0 %reduce-scatter.10.cloned.1.call-start = ((), (), s32[]{:S(2)}) async-start(), calls=%async_computation.5 | async-start | bytes 1179648 | tf_op jit(solution)/shard_map/reduce_scatter | solution.py:59
  159.5 13.7 %copy-start.2 = (bf16[128,16,128]{2,1,0:T(8,128)(2,1)S(1)}, bf16[128,16,128]{2,1,0:T(8,128)(2,1)}, u32[]{:S(2)}) copy-start(bf16[128,16,128]{2,1,0:T(8,128)(2,1)} %param.9) | copy-start | bytes 1572868
  159.5 127.8 %reduce-scatter.14.cloned.1.call-start = ((), (), s32[]{:S(2)}) async-start(), calls=%async_computation.7 | async-start | bytes 73728 | tf_op jit(solution)/shard_map/reduce_scatter | solution.py:60
  173.1 137.8 %reduce-scatter.12.cloned.1.call-start = ((), (), s32[]{:S(2)}) async-start(), calls=%async_computation.6 | async-start | bytes 655360 | tf_op jit(solution)/shard_map/reduce_scatter | solution.py:62
Sparse Core Ops, SparseCore 0:
  16.8 24.3 reduce-scatter.15
  128.1 17.9 reduce-scatter.17
  159.6 62.3 reduce-scatter.9
  225.8 61.4 reduce-scatter.13
  290.2 20.6 reduce-scatter.11
